TPU v7x, 32 devices: a whole 2x2x4 slice. The times are simulated.
32 devices in a mesh: grp: 4 (over y, x), dev: 8 (over z, core).
Axes of the slice: x: 2, y: 2, z: 4, core: 2. Of those that a mesh axis runs over, the one named last changes fastest.
Arguments:
- queries: bfloat16 [4096, 256], P(('grp', 'dev')), may hold values from -32 to 32
- items: bfloat16 [4096, 256], P(('grp', 'dev')), may hold values from -24 to 24
- item_ids: int32 [4096], P('grp'), may hold values from 0 to 262143
- neg_embed: bfloat16 [4096, 256], P('dev'), may hold values from -6 to 6
- neg_logq: float32 [4096], P('dev'), may hold values from -12 to -8
- logq_table: float32 [262144], replicated, may hold values from -11 to -9.5
Outputs:
- query_loss: float32 [4096], P(('grp', 'dev'))
- query_grad: float32 [4096, 256], P(('grp', 'dev'))
- item_grad: float32 [4096, 256], P(('grp', 'dev'))
- negative_grad: float32 [4096, 256], P('dev')
Inputs may be any that keep to these rules, and one draw needn't show every extreme that they name: `item_ids`: a row of logq_table.
All inputs are finite; a program needn't handle non-finite values.
Results may differ from a plain program's by a relative error of at most 0.0036.
Values may be sent and summed in bfloat16 or wider, within the bound.
No kernel may reach another device: no remote copies, remote signals or barrier semaphores. Data moves between devices by JAX's collectives and lax.ppermute only.
A program may use at most 64 MiB of HBM per device.

v0:
```python
import jax
import jax.numpy as jnp
from jax import lax
from jax.sharding import PartitionSpec as P

logit_scale = 0.25


def block_shape(all_rows):
    block_rows = min(512, all_rows)
    return (block_rows, all_rows // block_rows)


def log_total(maxima, totals):
    row_max = lax.pmax(maxima, "dev")
    row_sum = lax.psum(totals * jnp.exp(maxima - row_max), "dev")
    return row_max + jnp.log(row_sum)


def row_stats(scores):
    row_max = jnp.max(scores, axis=1)
    return (row_max, jnp.sum(jnp.exp(scores - row_max[:, None]), axis=1))


def logits(q_block, candidates, cand_offsets):
    return (
        logit_scale * jnp.dot(q_block, candidates.T, preferred_element_type=jnp.float32)
        - cand_offsets[None, :]
    )


def local(queries, items, item_ids, neg_embed, neg_logq, logq_table):
    own_rows, feat_width = queries.shape
    dev_index = lax.axis_index("dev")
    own_start = dev_index * own_rows
    own_ids = lax.dynamic_slice_in_dim(item_ids, own_start, own_rows, 0)
    own_offsets = jnp.take(logq_table, own_ids, axis=0)
    group_q = lax.all_gather(queries, "dev", axis=0, tiled=True)
    all_rows = group_q.shape[0]
    block_rows, block_count = block_shape(all_rows)
    blocks = group_q.reshape(block_count, block_rows, feat_width)
    starts = jnp.arange(block_count, dtype=jnp.int32) * block_rows
    candidates = jnp.concatenate([items, neg_embed], axis=0)
    cand_offsets = jnp.concatenate([own_offsets, neg_logq], axis=0)
    columns = jnp.arange(candidates.shape[0], dtype=jnp.int32)

    def positives(first_row):
        targets = first_row + jnp.arange(block_rows, dtype=jnp.int32) - own_start
        return (columns[None, :] == targets[:, None]) & (columns[None, :] < own_rows)

    def forward(packed):
        q_block, first_row = packed
        scores = logits(q_block, candidates, cand_offsets)
        row_max, row_sum = row_stats(scores)
        return (row_max, row_sum, jnp.sum(jnp.where(positives(first_row), scores, 0.0), axis=1))

    maxima, totals, matched = lax.map(forward, (blocks, starts))
    log_norm = log_total(maxima.reshape(all_rows), totals.reshape(all_rows))
    own_norm = lax.dynamic_slice_in_dim(log_norm, own_start, own_rows, 0)
    own_match = lax.dynamic_slice_in_dim(matched.reshape(all_rows), own_start, own_rows, 0)
    query_loss = own_norm - own_match

    def backward(summed, packed):
        q_block, first_row, block_norm = packed
        scores = logits(q_block, candidates, cand_offsets)
        logit_grad = (
            logit_scale
            * (jnp.exp(scores - block_norm[:, None]) - positives(first_row).astype(jnp.float32))
        ).astype(jnp.bfloat16)
        summed = summed + jnp.einsum(
            "rc,rd->cd", logit_grad, q_block, preferred_element_type=jnp.float32
        )
        return (summed, jnp.dot(logit_grad, candidates, preferred_element_type=jnp.float32))

    zero_acc = jnp.zeros((candidates.shape[0], feat_width), jnp.float32)
    cand_grad, q_partial = lax.scan(
        backward, zero_acc, (blocks, starts, log_norm.reshape(block_count, block_rows))
    )
    query_grad = lax.psum_scatter(
        q_partial.reshape(all_rows, feat_width), "dev", scatter_dimension=0, tiled=True
    )
    item_grad = cand_grad[:own_rows]
    negative_part = cand_grad[own_rows:]
    negative_grad = lax.psum(negative_part, "grp")
    return (query_loss, query_grad, item_grad, negative_grad)


def solution(mesh):
    return jax.shard_map(
        local,
        mesh=mesh,
        in_specs=(
            P(("grp", "dev"), None),
            P(("grp", "dev"), None),
            P("grp"),
            P("dev", None),
            P("dev"),
            P(),
        ),
        out_specs=(
            P(("grp", "dev")),
            P(("grp", "dev"), None),
            P(("grp", "dev"), None),
            P("dev", None),
        ),
        check_vma=False,
    )
```

profile of v0, /device:TPU:0, one launch (start us, length us, event | category | flops | bytes accessed | tf_op | source)
XLA Modules:
  0.0 128.1 jit_solution(7890898230688318742)
XLA Ops:
  8.0 0.0 copy-start
  8.0 0.0 copy-start.3
  8.0 0.0 all-reduce.2.cloned.1.call-start
  8.1 0.8 compare_select_fusion
  9.0 0.3 copy-done
  9.2 1.1 gather_fusion
  10.4 0.8 and_select_fusion
  11.2 0.8 constant_dynamic-update-slice_fusion.1
  12.0 16.7 %all_gather.3 = bf16[1024,256]{1,0:T(8,128)(2,1)S(1)} all-gather(bf16[128,256]{1,0:T(8,128)(2,1)} %param.10), channel_id=1, replica_groups=mesh['grp'=4,'dev'=8] {'dev'}, dimensions={0}, use_global_device_ids=true | all-gather | bytes 589824 | tf_op jit(solution)/shard_map/all_gather | solution.py:38
  28.7 0.7 pad_maximum_fusion
  29.4 0.0 copy-done.3
  29.4 5.2 %while.30 = (s32[]{:T(128)}, f32[2,512]{1,0:T(2,128)S(1)}, f32[2,512]{1,0:T(2,128)S(1)}, f32[2,512]{1,0:T(2,128)S(1)}, bf16[2,512,256]{2,1,0:T(8,128)(2,1)S(1)},...) while((s32[]{:T(128)}, f32[2,512]{1,0:T(2,128)S(1)}, ...), condition=%wide.region_4.5_spmd.clone.clone, body=%wide.region_0.4_spmd.clone.clone.sunk | while | flops 170721408 | bytes 3241369 | solution.py:57
  29.4 0.6 dynamic_slice.67
  30.0 0.6 add_subtract_fusion.4
  30.7 0.5 fusion.40
  31.2 0.7 select_reduce_fusion.2
  32.0 0.6 dynamic_slice.67
  32.6 0.6 add_subtract_fusion.4
  33.3 0.5 fusion.40
  33.8 0.7 select_reduce_fusion.2
  34.6 17.0 %pmax.7 = f32[1024]{0:T(1024)S(1)} all-reduce(f32[1024]{0:T(1024)S(1)} %bitcast.69), channel_id=1, replica_groups=mesh['grp'=4,'dev'=8] {'dev'}, use_global_device_ids=true, to_apply=%region_5.6 | all-reduce | flops 1024 | bytes 8192 | tf_op jit(solution)/shard_map/pmax | solution.py:15
  51.6 13.6 %psum.14 = f32[1024]{0:T(1024)S(1)} all-reduce(f32[1024]{0:T(1024)S(1)} %exponential_multiply_fusion), channel_id=1, replica_groups=mesh['grp'=4,'dev'=8] {'dev'}, use_global_device_ids=true, to_apply=%region_6.7 | all-reduce | flops 1024 | bytes 8192 | tf_op jit(solution)/shard_map/psum | solution.py:16
  65.2 9.0 %while.31 = (s32[]{:T(128)}, f32[640,256]{1,0:T(8,128)S(1)}, f32[2,512,256]{2,1,0:T(8,128)}, bf16[2,512,256]{2,1,0:T(8,128)(2,1)S(1)}, bf16[640,256]{1,0:T(8,128...) while((s32[]{:T(128)}, f32[640,256]{1,0:T(8,128)S(1)}, ...), condition=%wide.region_8.9_spmd.clone.clone, body=%wide.region_7.8_spmd.clone.clone.sunk | while | flops 506594944 | bytes 13385563 | solution.py:76
  65.2 0.6 dynamic_slice.71
  65.8 0.6 add_subtract_fusion.5
  66.5 0.6 fusion.47
  67.1 0.0 copy-start.1
  67.1 0.5 convolution_add_fusion.2
  67.7 0.7 copy-done.1
  68.4 0.4 fusion.48
  68.7 0.0 copy-start.2
  68.7 1.0 copy-done.2
  69.7 0.6 dynamic_slice.71
  70.3 0.6 add_subtract_fusion.5
  71.0 0.6 fusion.47
  71.6 0.0 copy-start.1
  71.6 0.5 convolution_add_fusion.2
  72.2 0.7 copy-done.1
  72.9 0.4 fusion.48
  73.2 0.0 copy-start.2
  73.2 1.0 copy-done.2
  74.2 0.8 slice.7
  75.0 0.0 all-reduce.2.cloned.1.call-update
  75.1 0.0 reduce-scatter.2.cloned.1.call-start
  75.1 0.5 reduce-scatter.2.cloned.1.call-update
  75.7 0.7 slice.6
  76.3 0.6 dynamic-slice_subtract_fusion
  76.9 41.9 %all-reduce.2.cloned.1.call-done = f32[512,256]{1,0:T(8,128)} async-done(((f32[512,256]{1,0:T(8,128)}), f32[512,256]{1,0:T(8,128)}) %all-reduce.2.cloned.1.call-update) | async-done | bytes 524304 | tf_op jit(solution)/shard_map/psum | solution.py:84
  118.8 0.0 reduce-scatter.2.cloned.1.call-done
  118.8 1.9 %copy.40 = f32[512,256]{1,0:T(8,128)} copy(f32[512,256]{1,0:T(8,128)} %all-reduce.2.cloned.1.call-done) | data formatting | bytes 1048576
  (26 shorter events, 0.4 us)
Async XLA Ops:
  8.0 1.2 copy-start
  8.0 21.4 %copy-start.3 = (bf16[512,256]{1,0:T(8,128)(2,1)S(1)}, bf16[512,256]{1,0:T(8,128)(2,1)}, u32[]{:S(2)}) copy-start(bf16[512,256]{1,0:T(8,128)(2,1)} %param.13) | copy-start | bytes 786436
  8.0 110.8 %all-reduce.2.cloned.1.call-start = ((), (), s32[]{:S(2)}) async-start(), calls=%async_computation.2 | async-start | bytes 1048576 | tf_op jit(solution)/shard_map/psum | solution.py:84
  67.1 1.2 copy-start.1
  68.7 1.0 copy-start.2
  71.6 1.2 copy-start.1
  73.2 1.0 copy-start.2
  75.1 43.7 %reduce-scatter.2.cloned.1.call-start = ((), (), s32[]{:S(2)}) async-start(), calls=%async_computation.1 | async-start | bytes 1179648 | tf_op jit(solution)/shard_map/reduce_scatter | solution.py:79
Sparse Core Ops, SparseCore 0:
  75.2 43.5 all-reduce.1
Sparse Core Ops, SparseCore 1:
  78.4 30.7 reduce-scatter.1
where the time goes:
time: 129 us; the launch traced here: 128 us
  blocking collectives  47.3 us (37%)
  waiting for transfers between devices  42.4 us (33%)
  between operations  15.6 us (12%)
  local copies, waits for them, and re-layouts  11.6 us (9%)
  other arithmetic  6.94 us (5%)
  matrix products  4.02 us (3%)
    psum x1, waiting for transfers between devices, local(): negative_grad = lax.psum(negative_part, 'grp')  41.9 us
    pmax x1, blocking collectives, log_total(): row_max = lax.pmax(maxima, 'dev')  17 us
    all_gather x1, blocking collectives, local(): group_q = lax.all_gather(queries, 'dev', axis=0, tiled=True)  16.7 us
    psum x1, blocking collectives, log_total(): row_sum = lax.psum(totals * jnp.exp(maxima - row_max), 'dev')  13.6 us
    while x8, local copies, waits for them, and re-layouts  3.35 us
    unnamed x9, local copies, waits for them, and re-layouts  2.99 us
    sub x4, other arithmetic, positives(): targets = first_row + jnp.arange(block_rows, dtype=jnp.int32) - own_start  2.59 us
  transfers between devices with their start and end apart: 2, of which 1 were waited for; matrix products, arithmetic and copies ran while one was open for 1% of the time, Pallas kernels for 0%

commit v1 on v0

--- a/solution.py
+++ b/solution.py
@@ -81,7 +81,11 @@
     )
     item_grad = cand_grad[:own_rows]
     negative_part = cand_grad[own_rows:]
-    negative_grad = lax.psum(negative_part, "grp")
+    negative_grad = negative_part
+    for hop in (1, 2):
+        negative_grad = negative_grad + lax.ppermute(
+            negative_grad, "grp", [(dev, dev ^ hop) for dev in range(4)]
+        )
     return (query_loss, query_grad, item_grad, negative_grad)
 
 

time: 129 us -> 112 us (0.87)
  waiting for transfers between devices: 42.4 us -> 25.6 us
  starting transfers between devices: 0.08 us -> 3.18 us
  local copies, waits for them, and re-layouts: 11.6 us -> 8.96 us
  between operations: 15.6 us -> 14.2 us
    psum x1 -> x0, waiting for transfers between devices: 41.9 us -> none  [local(): negative_grad = lax.psum(negative_part, 'grp')]
    ppermute x0 -> x2, waiting for transfers between devices: none -> 22.3 us  [local(): lax.ppermute(negative_grad, 'grp', [(dev, dev ^ hop) for dev in range(4)])]
    reduce_scatter x1, waiting for transfers between devices: 0.01 us -> 3.29 us  [local(): lax.psum_scatter(q_partial.reshape(all_rows, feat_width), 'dev', scatter_...]
    ppermute x0 -> x2, starting transfers between devices: none -> 3.14 us  [local(): lax.ppermute(negative_grad, 'grp', [(dev, dev ^ hop) for dev in range(4)])]
    unnamed x9 -> x8, local copies, waits for them, and re-layouts: 2.99 us -> 1.12 us
  transfers between devices with their start and end apart: 2 -> 3, of which waited for: 1 -> 3; matrix products, arithmetic and copies ran while one was open for 1% -> 2% of each run, Pallas kernels for 0% -> 0%
where the time goes in v1:
time: 112 us; the launch traced here: 111 us
  blocking collectives  47.3 us (42%)
  waiting for transfers between devices  25.6 us (23%)
  between operations  14.2 us (13%)
  local copies, waits for them, and re-layouts  8.96 us (8%)
  other arithmetic  7.87 us (7%)
  matrix products  4.03 us (4%)
  starting transfers between devices  3.18 us (3%)
    ppermute x2, waiting for transfers between devices, local(): lax.ppermute(negative_grad, 'grp', [(dev, dev ^ hop) for dev in range(4)])  22.3 us
    pmax x1, blocking collectives, log_total(): row_max = lax.pmax(maxima, 'dev')  17 us
    all_gather x1, blocking collectives, local(): group_q = lax.all_gather(queries, 'dev', axis=0, tiled=True)  16.7 us
    psum x1, blocking collectives, log_total(): row_sum = lax.psum(totals * jnp.exp(maxima - row_max), 'dev')  13.6 us
    while x8, local copies, waits for them, and re-layouts  3.35 us
    reduce_scatter x1, waiting for transfers between devices, local(): lax.psum_scatter(q_partial.reshape(all_rows, feat_width), 'dev', scatter_...  3.29 us
    ppermute x2, starting transfers between devices, local(): lax.ppermute(negative_grad, 'grp', [(dev, dev ^ hop) for dev in range(4)])  3.14 us
    sub x4, other arithmetic, positives(): targets = first_row + jnp.arange(block_rows, dtype=jnp.int32) - own_start  2.59 us
  transfers between devices with their start and end apart: 3, of which 3 were waited for; matrix products, arithmetic and copies ran while one was open for 2% of the time, Pallas kernels for 0%

profile of v1, /device:TPU:0, one launch (start us, length us, event | category | flops | bytes accessed | tf_op | source)
XLA Modules:
  0.0 111.2 jit_solution(10711999760987001883)
XLA Ops:
  7.2 0.0 copy-start
  7.2 0.0 copy-start.3
  7.2 0.0 reduce-scatter.2.cloned.1.call-start
  7.3 0.8 compare_select_fusion
  8.2 0.3 copy-done
  8.4 1.1 %gather_fusion = f32[128]{0:T(128)S(1)} fusion(f32[262144]{0:T(1024)S(1)} %copy-done, s32[1024]{0:T(1024)S(1)} %pad_clamp_fusion), kind=kCustom, calls=%fused_computation | custom fusion | bytes 1536 | tf_op jit(solution)/shard_map/jit(_take)/gather | solution.py:37
  9.6 0.8 and_select_fusion
  10.3 0.8 constant_dynamic-update-slice_fusion.1
  11.2 16.7 %all_gather.3 = bf16[1024,256]{1,0:T(8,128)(2,1)S(1)} all-gather(bf16[128,256]{1,0:T(8,128)(2,1)} %param.10), channel_id=1, replica_groups=mesh['grp'=4,'dev'=8] {'dev'}, dimensions={0}, use_global_device_ids=true | all-gather | bytes 589824 | tf_op jit(solution)/shard_map/all_gather | solution.py:38
  27.9 0.7 pad_maximum_fusion
  28.6 0.0 copy-done.3
  28.6 5.2 %while.30 = (s32[]{:T(128)}, f32[2,512]{1,0:T(2,128)S(1)}, f32[2,512]{1,0:T(2,128)S(1)}, f32[2,512]{1,0:T(2,128)S(1)}, bf16[2,512,256]{2,1,0:T(8,128)(2,1)S(1)},...) while((s32[]{:T(128)}, f32[2,512]{1,0:T(2,128)S(1)}, ...), condition=%wide.region_4.5_spmd.clone.clone, body=%wide.region_0.4_spmd.clone.clone.sunk | while | flops 170721408 | bytes 3241369 | solution.py:57
  28.6 0.6 dynamic_slice.67
  29.2 0.6 add_subtract_fusion.4
  29.8 0.5 fusion.40
  30.3 0.7 select_reduce_fusion.2
  31.2 0.6 dynamic_slice.67
  31.8 0.6 add_subtract_fusion.4
  32.4 0.5 fusion.40
  32.9 0.7 select_reduce_fusion.2
  33.8 17.0 %pmax.7 = f32[1024]{0:T(1024)S(1)} all-reduce(f32[1024]{0:T(1024)S(1)} %bitcast.69), channel_id=1, replica_groups=mesh['grp'=4,'dev'=8] {'dev'}, use_global_device_ids=true, to_apply=%region_5.6 | all-reduce | flops 1024 | bytes 8192 | tf_op jit(solution)/shard_map/pmax | solution.py:15
  50.8 13.6 %psum.7 = f32[1024]{0:T(1024)S(1)} all-reduce(f32[1024]{0:T(1024)S(1)} %exponential_multiply_fusion), channel_id=1, replica_groups=mesh['grp'=4,'dev'=8] {'dev'}, use_global_device_ids=true, to_apply=%region_6.7 | all-reduce | flops 1024 | bytes 8192 | tf_op jit(solution)/shard_map/psum | solution.py:16
  64.4 9.0 %while.31 = (s32[]{:T(128)}, f32[640,256]{1,0:T(8,128)S(1)}, f32[2,512,256]{2,1,0:T(8,128)}, bf16[2,512,256]{2,1,0:T(8,128)(2,1)S(1)}, bf16[640,256]{1,0:T(8,128...) while((s32[]{:T(128)}, f32[640,256]{1,0:T(8,128)S(1)}, ...), condition=%wide.region_8.9_spmd.clone.clone, body=%wide.region_7.8_spmd.clone.clone.sunk | while | flops 506594944 | bytes 13385563 | solution.py:76
  64.4 0.6 dynamic_slice.71
  65.0 0.6 add_subtract_fusion.5
  65.7 0.6 fusion.47
  66.3 0.0 copy-start.1
  66.3 0.5 convolution_add_fusion.2
  66.8 0.7 copy-done.1
  67.5 0.4 fusion.48
  67.9 0.0 copy-start.2
  67.9 1.0 copy-done.2
  68.9 0.6 dynamic_slice.71
  69.5 0.6 add_subtract_fusion.5
  70.2 0.6 fusion.47
  70.8 0.0 copy-start.1
  70.8 0.5 convolution_add_fusion.2
  71.3 0.7 copy-done.1
  72.0 0.4 fusion.48
  72.4 0.0 copy-start.2
  72.4 1.0 copy-done.2
  73.4 0.0 reduce-scatter.2.cloned.1.call-update
  73.5 1.6 %collective-permute-start = (f32[512,256]{1,0:T(8,128)S(1)}, f32[512,256]{1,0:T(8,128)S(1)}, u32[]{:S(2)}, u32[]{:S(2)}) collective-permute-start(f32[512,256]{1,0:T(8,128)S(1)} %slice.7), channel_id=1, source_target_pairs={{0,8},{8,0},{16,24},{24,16},{1,9},{9,1},{17,25},{25,17},{2,10},{10... | collective-permute-start | bytes 1572872 | tf_op jit(solution)/shard_map/ppermute | solution.py:86
  75.0 12.2 %collective-permute-done = f32[512,256]{1,0:T(8,128)S(1)} collective-permute-done((f32[512,256]{1,0:T(8,128)S(1)}, f32[512,256]{1,0:T(8,128)S(1)}, u32[]{:S(2)}, u32[]{:S(2)}) %collective-permute-start) | collective-permute-done | bytes 524320 | tf_op jit(solution)/shard_map/ppermute | solution.py:86
  87.2 0.1 slice_add_fusion
  87.3 1.6 %collective-permute-start.1 = (f32[512,256]{1,0:T(8,128)S(1)}, f32[512,256]{1,0:T(8,128)S(1)}, u32[]{:S(2)}, u32[]{:S(2)}) collective-permute-start(f32[512,256]{1,0:T(8,128)S(1)} %slice_add_fusion), channel_id=1, source_target_pairs={{0,16},{8,24},{16,0},{24,8},{1,17},{9,25},{17,1},{25,9},{2,18},{10... | collective-permute-start | bytes 1572872 | tf_op jit(solution)/shard_map/ppermute | solution.py:86
  88.9 0.7 slice.6
  89.6 0.6 dynamic-slice_subtract_fusion
  90.2 10.1 %collective-permute-done.1 = f32[512,256]{1,0:T(8,128)S(1)} collective-permute-done((f32[512,256]{1,0:T(8,128)S(1)}, f32[512,256]{1,0:T(8,128)S(1)}, u32[]{:S(2)}, u32[]{:S(2)}) %collective-permute-start.1) | collective-permute-done | bytes 524320 | tf_op jit(solution)/shard_map/ppermute | solution.py:86
  100.2 0.9 add.60
  101.1 3.3 %reduce-scatter.2.cloned.1.call-done = f32[128,256]{1,0:T(8,128)} async-done(((f32[1024,256]{1,0:T(8,128)}), f32[128,256]{1,0:T(8,128)}) %reduce-scatter.2.cloned.1.call-update) | async-done | bytes 131088 | tf_op jit(solution)/shard_map/reduce_scatter | solution.py:79
  (27 shorter events, 0.4 us)
Async XLA Ops:
  7.2 1.2 %copy-start = (f32[262144]{0:T(1024)S(1)}, f32[262144]{0:T(1024)}, u32[]{:S(2)}) copy-start(f32[262144]{0:T(1024)} %param.15) | copy-start | bytes 3145732
  7.2 21.4 %copy-start.3 = (bf16[512,256]{1,0:T(8,128)(2,1)S(1)}, bf16[512,256]{1,0:T(8,128)(2,1)}, u32[]{:S(2)}) copy-start(bf16[512,256]{1,0:T(8,128)(2,1)} %param.13) | copy-start | bytes 786436
  7.2 97.2 %reduce-scatter.2.cloned.1.call-start = ((), (), s32[]{:S(2)}) async-start(), calls=%async_computation.1 | async-start | bytes 1179648 | tf_op jit(solution)/shard_map/reduce_scatter | solution.py:79
  66.3 1.2 %copy-start.1 = (f32[2,512,256]{2,1,0:T(8,128)S(1)}, f32[2,512,256]{2,1,0:T(8,128)}, u32[]{:S(2)}) copy-start(f32[2,512,256]{2,1,0:T(8,128)} %get-tuple-element.426) | copy-start | bytes 3145732 | tf_op jit(solution)/shard_map/while
  67.9 1.0 copy-start.2
  70.8 1.2 %copy-start.1 = (f32[2,512,256]{2,1,0:T(8,128)S(1)}, f32[2,512,256]{2,1,0:T(8,128)}, u32[]{:S(2)}) copy-start(f32[2,512,256]{2,1,0:T(8,128)} %get-tuple-element.426) | copy-start | bytes 3145732 | tf_op jit(solution)/shard_map/while
  72.4 1.0 copy-start.2
  73.5 13.8 %collective-permute-start = (f32[512,256]{1,0:T(8,128)S(1)}, f32[512,256]{1,0:T(8,128)S(1)}, u32[]{:S(2)}, u32[]{:S(2)}) collective-permute-start(f32[512,256]{1,0:T(8,128)S(1)} %slice.7), channel_id=1, source_target_pairs={{0,8},{8,0},{16,24},{24,16},{1,9},{9,1},{17,25},{25,17},{2,10},{10... | collective-permute-start | bytes 1572872 | tf_op jit(solution)/shard_map/ppermute | solution.py:86
  87.3 12.9 %collective-permute-start.1 = (f32[512,256]{1,0:T(8,128)S(1)}, f32[512,256]{1,0:T(8,128)S(1)}, u32[]{:S(2)}, u32[]{:S(2)}) collective-permute-start(f32[512,256]{1,0:T(8,128)S(1)} %slice_add_fusion), channel_id=1, source_target_pairs={{0,16},{8,24},{16,0},{24,8},{1,17},{9,25},{17,1},{25,9},{2,18},{10... | collective-permute-start | bytes 1572872 | tf_op jit(solution)/shard_map/ppermute | solution.py:86
Sparse Core Ops, SparseCore 0:
  73.5 30.8 reduce-scatter.1
